TPU v7x, 128 devices: a whole 4x4x4 slice. The times are simulated.
128 devices in a mesh: tm: 128 (over z, x, y, core).
Axes of the slice: x: 4, y: 4, z: 4, core: 2. Of those that a mesh axis runs over, the one named last changes fastest.
Arguments:
- measurements: float32 [1024, 192, 512], P('tm'), may hold values from -8 to 8
- observed: int32 [1024], P('tm'), may hold values 0 or 1
- segment_ids: int32 [1024], P('tm'), may hold values from 0 to 31, never falling along the last dimension, each value on 1 to 64 neighbouring positions
- courant_table: float32 [32, 4], replicated, may hold values from 0.15 to 0.6
- filter_gains: float32 [192], replicated, may hold values from 0.0005 to 0.08
- initial_state: float32 [192, 512], replicated, may hold values from -6 to 6
Outputs:
- filtered: float32 [1024, 192, 512], P('tm')
- consistency: float32 [512], replicated
Inputs may be any that keep to these rules, and one draw needn't show every extreme that they name: `segment_ids`: the segment number never falls along time; each segment lasts 1 to 64 steps, one exactly that.
All inputs are finite; a program needn't handle non-finite values. No bound on the sum of `observed` on one device may be relied on, other than what follows from the above.
Results may differ from a plain program's by a relative error of at most 0.0003.
Values sent between devices are 32-bit elements; how exact they have to be, the bound alone decides.
A program may use at most 192 MiB of HBM per device.

v0:
```python
import jax
import jax.numpy as jnp
from jax import lax
from jax.sharding import PartitionSpec as P

CABLES = 4
HALF = 24
SEGS = 32
PAYLOAD = 0.3
HIGHEST = lax.Precision.HIGHEST


def prefix(part, axis, combine, identity):
    place = lax.axis_index(axis)
    gathered = jax.tree.map(lambda a: lax.all_gather(a, axis), part)
    state = jax.tree.map(lambda a, e: jnp.zeros_like(a) + jnp.asarray(e, a.dtype), part, identity)

    def one(turn, state):
        return combine(
            state, jax.tree.map(lambda a: lax.dynamic_index_in_dim(a, turn, 0, False), gathered)
        )

    return lax.fori_loop(0, place, one, state)


def coupling_pattern():
    count = CABLES * HALF
    indices = jnp.arange(count)
    cable_of = indices // HALF
    node_of = indices % HALF
    same = cable_of[:, None] == cable_of[None, :]
    lower = same & (indices[:, None] == indices[None, :] + 1)
    ends = (node_of[:, None] == HALF - 1) & (node_of[None, :] == HALF - 1) & jnp.logical_not(same)
    pattern = (
        jnp.eye(count, dtype=jnp.float32)
        - lower.astype(jnp.float32)
        - PAYLOAD * ends.astype(jnp.float32)
    )
    return (pattern, cable_of)


def transitions_from(courant):
    pattern, cable_of = coupling_pattern()
    member = (cable_of[:, None] == jnp.arange(CABLES)[None, :]).astype(jnp.float32)
    row_scale = jnp.einsum("sc,rc->sr", courant, member, precision=HIGHEST)
    coupled = row_scale[:, :, None] * pattern[None]
    gram = jnp.einsum("sji,sjk->sik", coupled, coupled, precision=HIGHEST)
    ident = jnp.broadcast_to(jnp.eye(pattern.shape[0], dtype=jnp.float32), coupled.shape)
    upper_rows = jnp.concatenate([ident - gram, -jnp.swapaxes(coupled, 1, 2)], axis=2)
    lower_rows = jnp.concatenate([coupled, ident], axis=2)
    return jnp.concatenate([upper_rows, lower_rows], axis=1)


def matmul(left, right):
    return jnp.dot(left, right, precision=HIGHEST, preferred_element_type=jnp.float32)


def compose(earlier, later):
    return (matmul(later[0], earlier[0]), matmul(later[0], earlier[1]) + later[1])


def local(measurements, observed, segment_ids, courant_table, filter_gains, initial_state):
    steps_here = measurements.shape[0]
    states = measurements.shape[1]
    flights = measurements.shape[2]
    selector = (segment_ids[:, None] == jnp.arange(SEGS)[None, :]).astype(jnp.float32)
    courant = jnp.dot(
        selector, courant_table, precision=HIGHEST, preferred_element_type=jnp.float32
    )
    transitions = transitions_from(courant)
    weights = observed.astype(jnp.float32)
    keep_factor = 1.0 - weights[:, None] * filter_gains[None, :]
    affine_maps = keep_factor[:, :, None] * transitions
    affine_shifts = weights[:, None, None] * filter_gains[None, :, None] * measurements
    identity_map = jnp.eye(states, dtype=jnp.float32)
    zero_shift = jnp.zeros((states, flights), jnp.float32)

    def fold_local(carry, element):
        return (compose(carry, element), None)

    (block_map, block_shift), unused = lax.scan(
        fold_local, (identity_map, zero_shift), (affine_maps, affine_shifts)
    )
    prefix_map, prefix_shift = prefix(
        (block_map, block_shift), "tm", compose, (identity_map, zero_shift)
    )
    start_state = matmul(prefix_map, initial_state) + prefix_shift

    def advance(state, inputs):
        transition, weight, sample = inputs
        predicted = matmul(transition, state)
        innovation = sample - predicted
        updated = predicted + weight * filter_gains[:, None] * innovation
        power = weight * jnp.sum(innovation * innovation, axis=0)
        return (updated, (updated, power))

    unused_state, (filtered, powers) = lax.scan(
        advance, start_state, (transitions, weights, measurements)
    )
    partial_power = jnp.sum(powers, axis=0)
    total_power = lax.psum(partial_power, "tm")
    consistency = total_power / (steps_here * lax.axis_size("tm") * states)
    return (filtered, consistency)


def solution(mesh):
    in_specs = (P("tm", None, None), P("tm"), P("tm"), P(), P(), P())
    out_specs = (P("tm", None, None), P())
    return jax.shard_map(local, mesh=mesh, in_specs=in_specs, out_specs=out_specs, check_vma=False)
```

profile of v0, /device:TPU:1, one launch (start us, length us, event | category | flops | bytes accessed | tf_op | source)
XLA Modules:
  0.0 762.9 jit_solution(17322322415439356978)
XLA Ops:
  7.3 0.9 fusion.26
  8.7 1.7 convolution_subtract_fusion
  10.4 0.7 convert_element_type.37
  11.1 0.8 broadcast_multiply_fusion.6
  11.8 3.9 broadcast_multiply_fusion.2
  15.8 1.7 maximum_maximum_fusion
  17.4 18.6 %while.41 = (s32[]{:T(128)}, f32[192,192]{1,0:T(8,128)S(1)}, f32[192,512]{1,0:T(8,128)S(1)}, f32[8,192,192]{1,2,0:T(8,128)S(1)}, f32[8,192,512]{2,1,0:T(8,128)}, /*index=5*/s32[]{:T(128)}, s32[]{:T(128)}) while((s32[]{:T(128)}, f32[192,192]{1,0:T(8,128)S(1)}, f32[192,512]{1,0:T(8,128)S(1)}, f32[8,192,192]{1,2,0:T(8,128)S(1)}, ...), condition=%wide.region_1.2_spmd.clone, body=%wide.region_0.1_spmd.clone.sunk | while | flops 311623680 | bytes 2999387 | solution.py:81
  17.4 1.7 convolution_add_fusion.6
  19.8 1.7 convolution_add_fusion.6
  22.1 1.7 convolution_add_fusion.6
  24.4 1.7 convolution_add_fusion.6
  26.8 1.7 convolution_add_fusion.6
  29.1 1.7 convolution_add_fusion.6
  31.4 1.7 convolution_add_fusion.6
  33.8 1.7 convolution_add_fusion.6
  36.1 0.7 copy-done.2
  36.9 0.6 all-gather.7.cloned.1.call-update
  37.5 96.1 %all-gather.5.cloned.1.call-done = f32[24576,192]{1,0:T(8,128)} async-done(((f32[192,192]{1,0:T(8,128)}), f32[24576,192]{1,0:T(8,128)}) %all-gather.5.cloned.1.call-update) | async-done | bytes 18874384 | tf_op jit(solution)/shard_map/all_gather | solution.py:15
  133.6 137.3 %all-gather.7.cloned.1.call-done = f32[24576,512]{1,0:T(8,128)} async-done(((f32[192,512]{1,0:T(8,128)}), f32[24576,512]{1,0:T(8,128)}) %all-gather.7.cloned.1.call-update) | async-done | bytes 50331664 | tf_op jit(solution)/shard_map/all_gather | solution.py:15
  271.0 3.0 while.39
  271.1 1.6 convolution_add_fusion.5
  272.7 1.2 fusion.52
  274.5 45.3 %while.40 = (s32[]{:T(128)}, f32[192,512]{1,0:T(8,128)S(1)}, f32[8,192,512]{2,1,0:T(8,128)}, f32[8,512]{1,0:T(8,128)S(1)}, f32[8,192,192]{1,2,0:T(8,128)}, /*ind...) while((s32[]{:T(128)}, f32[192,512]{1,0:T(8,128)S(1)}, ...), condition=%wide.region_6.7_spmd, body=%wide.region_4.6_spmd.sunk | while | flops 227082432 | bytes 3749249 | solution.py:97
  274.5 0.7 dynamic_slice.72
  275.2 0.6 broadcast_multiply_fusion.10
  275.8 2.5 bitcast_dynamic-update-slice_fusion.2
  278.4 1.1 multiply_reduce_fusion.2
  279.5 0.6 broadcast_multiply_fusion.11
  280.2 0.7 dynamic_slice.72
  280.8 0.6 broadcast_multiply_fusion.10
  281.5 2.5 bitcast_dynamic-update-slice_fusion.2
  284.0 1.1 multiply_reduce_fusion.2
  285.1 0.6 broadcast_multiply_fusion.11
  285.8 0.7 dynamic_slice.72
  286.5 0.6 broadcast_multiply_fusion.10
  287.2 2.5 bitcast_dynamic-update-slice_fusion.2
  289.7 1.1 multiply_reduce_fusion.2
  290.8 0.6 broadcast_multiply_fusion.11
  291.5 0.7 dynamic_slice.72
  292.2 0.6 broadcast_multiply_fusion.10
  292.8 2.5 bitcast_dynamic-update-slice_fusion.2
  295.4 1.1 multiply_reduce_fusion.2
  296.5 0.6 broadcast_multiply_fusion.11
  297.2 0.7 dynamic_slice.72
  297.8 0.6 broadcast_multiply_fusion.10
  298.5 2.5 bitcast_dynamic-update-slice_fusion.2
  301.0 1.1 multiply_reduce_fusion.2
  302.1 0.6 broadcast_multiply_fusion.11
  302.8 0.7 dynamic_slice.72
  303.5 0.6 broadcast_multiply_fusion.10
  304.2 2.5 bitcast_dynamic-update-slice_fusion.2
  306.7 1.1 multiply_reduce_fusion.2
  307.8 0.6 broadcast_multiply_fusion.11
  308.5 0.7 dynamic_slice.72
  309.2 0.6 broadcast_multiply_fusion.10
  309.8 2.5 bitcast_dynamic-update-slice_fusion.2
  312.4 1.1 multiply_reduce_fusion.2
  313.5 0.6 broadcast_multiply_fusion.11
  314.2 0.7 dynamic_slice.72
  314.8 0.6 broadcast_multiply_fusion.10
  315.5 2.5 bitcast_dynamic-update-slice_fusion.2
  318.0 1.1 multiply_reduce_fusion.2
  319.1 0.6 broadcast_multiply_fusion.11
  319.9 435.6 %psum.7 = f32[512]{0:T(512)S(1)} all-reduce(f32[512]{0:T(512)S(1)} %reduce_sum.18), channel_id=1, replica_groups=mesh['tm'=128] {'tm'}, use_global_device_ids=true, to_apply=%region_8.9 | all-reduce | flops 512 | bytes 4096 | tf_op jit(solution)/shard_map/psum | solution.py:101
  (70 shorter events, 7.7 us)
Async XLA Ops:
  7.2 266.8 %copy-start = (f32[192,512]{1,0:T(8,128)S(1)}, f32[192,512]{1,0:T(8,128)}, u32[]{:S(2)}) copy-start(f32[192,512]{1,0:T(8,128)} %param.17) | copy-start | bytes 1179652
  7.2 126.5 %all-gather.5.cloned.1.call-start = ((), (), s32[]{:S(2)}) async-start(), calls=%async_computation | async-start | bytes 25362432 | tf_op jit(solution)/shard_map/all_gather | solution.py:15
  11.8 3.9 copy-start.3
  36.1 0.7 copy-start.2
  36.1 0.8 copy-start.1
  36.8 234.2 %all-gather.7.cloned.1.call-start = ((), (), s32[]{:S(2)}) async-start(), calls=%async_computation.1 | async-start | bytes 50724864 | tf_op jit(solution)/shard_map/all_gather | solution.py:15
  271.0 3.5 copy-start.4
Sparse Core Ops, SparseCore 0:
  36.9 96.7 all-gather.4
  136.8 134.1 all-gather.6
where the time goes:
time: 770 us; the launch traced here: 763 us
  blocking collectives  436 us (57%)
  waiting for transfers between devices  234 us (30%)
  matrix products  44.5 us (6%)
  other arithmetic  26.6 us (3%)
  between operations  14.2 us (2%)
    psum x1, blocking collectives, local(): total_power = lax.psum(partial_power, 'tm')  436 us
    all_gather x2, waiting for transfers between devices, prefix(): gathered = jax.tree.map(lambda a: lax.all_gather(a, axis), part)  233 us
    dot_general x27, matrix products, matmul(): jnp.dot(left, right, precision=HIGHEST, preferred_element_type=jnp.float32)  41.8 us
  transfers between devices with their start and end apart: 2, of which 2 were waited for; matrix products, arithmetic and copies ran while one was open for 0% of the time, Pallas kernels for 0%

commit v1 on v0

--- a/solution.py
+++ b/solution.py
@@ -98,7 +98,7 @@
         advance, start_state, (transitions, weights, measurements)
     )
     partial_power = jnp.sum(powers, axis=0)
-    total_power = lax.psum(partial_power, "tm")
+    total_power = jnp.sum(lax.all_gather(partial_power, "tm"), axis=0)
     consistency = total_power / (steps_here * lax.axis_size("tm") * states)
     return (filtered, consistency)
 

time: 770 us -> 739 us (0.960)
  blocking collectives: 436 us -> 405 us
    psum x1 -> x0, blocking collectives: 436 us -> none  [local(): total_power = lax.psum(partial_power, 'tm')]
    all_gather x0 -> x1, blocking collectives: none -> 405 us  [local(): total_power = jnp.sum(lax.all_gather(partial_power, 'tm'), axis=0)]
where the time goes in v1:
time: 739 us; the launch traced here: 732 us
  blocking collectives  405 us (55%)
  waiting for transfers between devices  234 us (32%)
  matrix products  44.5 us (6%)
  other arithmetic  26.8 us (4%)
  between operations  14.2 us (2%)
    all_gather x1, blocking collectives, local(): total_power = jnp.sum(lax.all_gather(partial_power, 'tm'), axis=0)  405 us
    all_gather x2, waiting for transfers between devices, prefix(): gathered = jax.tree.map(lambda a: lax.all_gather(a, axis), part)  233 us
    dot_general x27, matrix products, matmul(): jnp.dot(left, right, precision=HIGHEST, preferred_element_type=jnp.float32)  41.8 us
  transfers between devices with their start and end apart: 2, of which 2 were waited for; matrix products, arithmetic and copies ran while one was open for 0% of the time, Pallas kernels for 0%

profile of v1, /device:TPU:1, one launch (start us, length us, event | category | flops | bytes accessed | tf_op | source)
XLA Modules:
  0.0 732.2 jit_solution(2670355820252143725)
XLA Ops:
  7.3 0.9 fusion.26
  8.7 1.7 convolution_subtract_fusion
  10.4 0.7 convert_element_type.37
  11.1 0.8 broadcast_multiply_fusion.6
  11.8 3.9 broadcast_multiply_fusion.2
  15.8 1.7 maximum_maximum_fusion
  17.4 18.6 %while.41 = (s32[]{:T(128)}, f32[192,192]{1,0:T(8,128)S(1)}, f32[192,512]{1,0:T(8,128)S(1)}, f32[8,192,192]{1,2,0:T(8,128)S(1)}, f32[8,192,512]{2,1,0:T(8,128)}, /*index=5*/s32[]{:T(128)}, s32[]{:T(128)}) while((s32[]{:T(128)}, f32[192,192]{1,0:T(8,128)S(1)}, f32[192,512]{1,0:T(8,128)S(1)}, f32[8,192,192]{1,2,0:T(8,128)S(1)}, ...), condition=%wide.region_1.2_spmd.clone, body=%wide.region_0.1_spmd.clone.sunk | while | flops 311623680 | bytes 2999387 | solution.py:81
  17.4 1.7 convolution_add_fusion.6
  19.8 1.7 convolution_add_fusion.6
  22.1 1.7 convolution_add_fusion.6
  24.4 1.7 convolution_add_fusion.6
  26.8 1.7 convolution_add_fusion.6
  29.1 1.7 convolution_add_fusion.6
  31.4 1.7 convolution_add_fusion.6
  33.8 1.7 convolution_add_fusion.6
  36.1 0.7 copy-done.2
  36.9 0.6 all-gather.9.cloned.1.call-update
  37.5 96.1 %all-gather.7.cloned.1.call-done = f32[24576,192]{1,0:T(8,128)} async-done(((f32[192,192]{1,0:T(8,128)}), f32[24576,192]{1,0:T(8,128)}) %all-gather.7.cloned.1.call-update) | async-done | bytes 18874384 | tf_op jit(solution)/shard_map/all_gather | solution.py:15
  133.6 137.3 %all-gather.9.cloned.1.call-done = f32[24576,512]{1,0:T(8,128)} async-done(((f32[192,512]{1,0:T(8,128)}), f32[24576,512]{1,0:T(8,128)}) %all-gather.9.cloned.1.call-update) | async-done | bytes 50331664 | tf_op jit(solution)/shard_map/all_gather | solution.py:15
  271.0 3.0 while.39
  271.1 1.6 convolution_add_fusion.5
  272.7 1.2 fusion.52
  274.5 45.3 %while.40 = (s32[]{:T(128)}, f32[192,512]{1,0:T(8,128)S(1)}, f32[8,192,512]{2,1,0:T(8,128)}, f32[8,512]{1,0:T(8,128)S(1)}, f32[8,192,192]{1,2,0:T(8,128)}, /*ind...) while((s32[]{:T(128)}, f32[192,512]{1,0:T(8,128)S(1)}, ...), condition=%wide.region_6.7_spmd, body=%wide.region_4.6_spmd.sunk | while | flops 227082432 | bytes 3749249 | solution.py:97
  274.5 0.7 dynamic_slice.72
  275.2 0.6 broadcast_multiply_fusion.10
  275.8 2.5 bitcast_dynamic-update-slice_fusion.2
  278.4 1.1 multiply_reduce_fusion.2
  279.5 0.6 broadcast_multiply_fusion.11
  280.2 0.7 dynamic_slice.72
  280.8 0.6 broadcast_multiply_fusion.10
  281.5 2.5 bitcast_dynamic-update-slice_fusion.2
  284.0 1.1 multiply_reduce_fusion.2
  285.1 0.6 broadcast_multiply_fusion.11
  285.8 0.7 dynamic_slice.72
  286.5 0.6 broadcast_multiply_fusion.10
  287.2 2.5 bitcast_dynamic-update-slice_fusion.2
  289.7 1.1 multiply_reduce_fusion.2
  290.8 0.6 broadcast_multiply_fusion.11
  291.5 0.7 dynamic_slice.72
  292.2 0.6 broadcast_multiply_fusion.10
  292.8 2.5 bitcast_dynamic-update-slice_fusion.2
  295.4 1.1 multiply_reduce_fusion.2
  296.5 0.6 broadcast_multiply_fusion.11
  297.2 0.7 dynamic_slice.72
  297.8 0.6 broadcast_multiply_fusion.10
  298.5 2.5 bitcast_dynamic-update-slice_fusion.2
  301.0 1.1 multiply_reduce_fusion.2
  302.1 0.6 broadcast_multiply_fusion.11
  302.8 0.7 dynamic_slice.72
  303.5 0.6 broadcast_multiply_fusion.10
  304.2 2.5 bitcast_dynamic-update-slice_fusion.2
  306.7 1.1 multiply_reduce_fusion.2
  307.8 0.6 broadcast_multiply_fusion.11
  308.5 0.7 dynamic_slice.72
  309.2 0.6 broadcast_multiply_fusion.10
  309.8 2.5 bitcast_dynamic-update-slice_fusion.2
  312.4 1.1 multiply_reduce_fusion.2
  313.5 0.6 broadcast_multiply_fusion.11
  314.2 0.7 dynamic_slice.72
  314.8 0.6 broadcast_multiply_fusion.10
  315.5 2.5 bitcast_dynamic-update-slice_fusion.2
  318.0 1.1 multiply_reduce_fusion.2
  319.1 0.6 broadcast_multiply_fusion.11
  319.9 404.7 %all-gather.3 = f32[128,1,512]{2,1,0:T(1,128)S(1)} all-gather(f32[1,1,512]{2,1,0:T(1,128)S(1)} %bitcast.77), channel_id=4, replica_groups=mesh['tm'=128] {'tm'}, dimensions={0}, use_global_device_ids=true | all-gather | bytes 264192 | tf_op jit(solution)/shard_map/all_gather | solution.py:101
  (71 shorter events, 7.9 us)
Async XLA Ops:
  7.2 266.8 %copy-start = (f32[192,512]{1,0:T(8,128)S(1)}, f32[192,512]{1,0:T(8,128)}, u32[]{:S(2)}) copy-start(f32[192,512]{1,0:T(8,128)} %param.17) | copy-start | bytes 1179652
  7.2 126.5 %all-gather.7.cloned.1.call-start = ((), (), s32[]{:S(2)}) async-start(), calls=%async_computation | async-start | bytes 25362432 | tf_op jit(solution)/shard_map/all_gather | solution.py:15
  11.8 3.9 copy-start.3
  36.1 0.7 copy-start.2
  36.1 0.8 copy-start.1
  36.8 234.2 %all-gather.9.cloned.1.call-start = ((), (), s32[]{:S(2)}) async-start(), calls=%async_computation.1 | async-start | bytes 50724864 | tf_op jit(solution)/shard_map/all_gather | solution.py:15
  271.0 3.5 copy-start.4
Sparse Core Ops, SparseCore 0:
  36.9 96.7 all-gather.6
  136.8 134.1 all-gather.8
